TPU v7x, 32 devices: a whole 2x2x4 slice. The times are simulated.
32 devices in a mesh: dp: 16 (over z, x, core), tensor: 2 (over y).
Axes of the slice: x: 2, y: 2, z: 4, core: 2. Of those that a mesh axis runs over, the one named last changes fastest.
Arguments:
- inputs: bfloat16 [2048, 2048], P('dp'), may hold values from -6 to 6
- segments: int32 [2048], P('dp'), may hold values from 0 to 1, as said below
- positions: int32 [2048], P('dp'), may hold values from 0 to 1999, as said below
- w_query: bfloat16 [2048, 2048], P('dp', 'tensor')
- w_key: bfloat16 [2048, 512], P('dp', 'tensor')
- w_value: bfloat16 [2048, 512], P('dp', 'tensor'), may hold values from -0.125 to 0.125
- w_out: bfloat16 [2048, 2048], P('dp', 'tensor'), may hold values from -0.5 to 0.5
- w_gate: bfloat16 [2048, 8192], P('dp', 'tensor'), may hold values from -0.125 to 0.125
- w_up: bfloat16 [2048, 8192], P('dp', 'tensor'), may hold values from -0.125 to 0.125
- w_down: bfloat16 [2048, 8192], P('dp', 'tensor'), may hold values from -0.125 to 0.125
- attn_gain: bfloat16 [2048], P('dp'), may hold values from 0.5 to 1.5
- mlp_gain: bfloat16 [2048], P('dp'), may hold values from 0.5 to 1.5
- out_grad: bfloat16 [2048, 2048], P('dp'), may hold values from -6 to 6
Outputs:
- output: bfloat16 [2048, 2048], P('dp')
- input_grad: float32 [2048, 2048], P('dp')
- query_grad: float32 [2048, 2048], P('dp', 'tensor')
- key_grad: float32 [2048, 512], P('dp', 'tensor')
- value_grad: float32 [2048, 512], P('dp', 'tensor')
- out_proj_grad: float32 [2048, 2048], P('dp', 'tensor')
- gate_grad: float32 [2048, 8192], P('dp', 'tensor')
- up_grad: float32 [2048, 8192], P('dp', 'tensor')
- down_grad: float32 [2048, 8192], P('dp', 'tensor')
- attn_gain_grad: float32 [2048], P('dp')
- mlp_gain_grad: float32 [2048], P('dp')
Inputs may be any that keep to these rules, and one draw needn't show every extreme that they name: `segments`: within each sequence of 128 tokens segment numbers start at 0 and rise by one where a document begins; documents span 200 to 2000 tokens of the packed stream, so a sequence's first document may have begun in the sequence before it. `positions`: A token's position within its document: it rises by one from token to token of a document and is 0 where a document begins; at a sequence's first token it continues a document that began earlier.
All inputs are finite; a program needn't handle non-finite values.
Results may differ from a plain program's by a relative error of at most 0.019.
The roundings to bfloat16 on the way count: a program that leaves them out, or rounds other values in their place, can miss the bound.
Values may be sent and summed in bfloat16 or wider, within the bound.
No kernel may reach another device: no remote copies, remote signals or barrier semaphores. Data moves between devices by JAX's collectives and lax.ppermute only.
A program may use at most 256 MiB of HBM per device.

v0:
```python
import math
import jax
import jax.numpy as jnp
from jax import lax
from jax.sharding import PartitionSpec as P

HEADS = 32
KV_HEADS = 8
HEAD_DIM = 64
norm_eps = 1e-05
rope_base = 500000.0
masked_score = -1e30


def rope_freqs(head_dim):
    index = jnp.arange(head_dim // 2, dtype=jnp.float32)
    inverse = rope_base ** (-2.0 * index / head_dim)
    wavelen = 2.0 * math.pi / inverse
    smooth = (8192.0 / wavelen - 1.0) / 3.0
    scaled = (1.0 - smooth) * inverse / 32.0 + smooth * inverse
    return jnp.where(wavelen < 2048.0, inverse, jnp.where(wavelen > 8192.0, inverse / 32.0, scaled))


def rotate(values, cosine, sine):
    half = values.shape[-1] // 2
    first = values[..., :half]
    second = values[..., half:]
    return jnp.concatenate(
        [first * cosine - second * sine, second * cosine + first * sine], axis=-1
    )


def norm_parts(values):
    scale = lax.rsqrt(jnp.mean(values * values, axis=-1, keepdims=True) + norm_eps)
    return (values * scale, scale)


def norm_back(grad, unit, scale, gain):
    weighted = grad * gain
    return (
        scale * (weighted - unit * jnp.mean(weighted * unit, axis=-1, keepdims=True)),
        jnp.sum(grad * unit, axis=0),
    )


def dot_last(left, right):
    return lax.dot_general(
        left, right, (((1,), (1,)), ((), ())), preferred_element_type=jnp.float32
    )


def dot_first(left, right):
    return lax.dot_general(
        left, right, (((0,), (0,)), ((), ())), preferred_element_type=jnp.float32
    )


def on_device(
    inputs,
    segments,
    positions,
    w_query,
    w_key,
    w_value,
    w_out,
    w_gate,
    w_up,
    w_down,
    attn_gain,
    mlp_gain,
    out_grad,
):
    length = inputs.shape[0]
    group = HEADS // KV_HEADS
    factor = HEAD_DIM ** (-0.5)
    residual = inputs.astype(jnp.float32)
    angle = positions.astype(jnp.float32)[:, None] * rope_freqs(HEAD_DIM)[None, :]
    cosine = jnp.cos(angle)[:, None, :]
    sine = jnp.sin(angle)[:, None, :]
    order = jnp.arange(length)
    allowed = (segments[:, None] == segments[None, :]) & (order[:, None] >= order[None, :])
    query_full, key_full, value_full, out_full, gain_one = (
        lax.all_gather(w_query, "dp", axis=0, tiled=True),
        lax.all_gather(w_key, "dp", axis=0, tiled=True),
        lax.all_gather(w_value, "dp", axis=0, tiled=True),
        lax.all_gather(w_out, "dp", axis=0, tiled=True),
        lax.all_gather(attn_gain, "dp", axis=0, tiled=True),
    )
    gain_one = gain_one.astype(jnp.float32)
    unit_one, scale_one = norm_parts(residual)
    normed_one = (unit_one * gain_one).astype(jnp.bfloat16)
    query_rot = rotate(
        jnp.dot(normed_one, query_full, preferred_element_type=jnp.float32).reshape(
            length, -1, HEAD_DIM
        ),
        cosine,
        sine,
    ).astype(jnp.bfloat16)
    key_rot = rotate(
        jnp.dot(normed_one, key_full, preferred_element_type=jnp.float32).reshape(
            length, -1, HEAD_DIM
        ),
        cosine,
        sine,
    ).astype(jnp.bfloat16)
    value_heads = (
        jnp.dot(normed_one, value_full, preferred_element_type=jnp.float32)
        .astype(jnp.bfloat16)
        .reshape(length, -1, HEAD_DIM)
    )
    kv_local = key_rot.shape[1]
    query_group = query_rot.reshape(length, kv_local, group, HEAD_DIM)
    scores = jnp.where(
        allowed,
        jnp.einsum("qhgd,khd->hgqk", query_group, key_rot, preferred_element_type=jnp.float32)
        * factor,
        masked_score,
    )
    top = jnp.max(scores, axis=-1, keepdims=True)
    expo = jnp.exp(scores - top)
    total = jnp.sum(expo, axis=-1, keepdims=True)
    log_total = top + jnp.log(total)
    weights_low = (expo / total).astype(jnp.bfloat16)
    attended = (
        jnp.einsum("hgqk,khd->qhgd", weights_low, value_heads, preferred_element_type=jnp.float32)
        .astype(jnp.bfloat16)
        .reshape(length, -1)
    )
    attn_out = lax.psum(dot_last(attended, out_full), "tensor")
    middle = residual + attn_out
    gate_full, up_full, down_full, gain_two = (
        lax.all_gather(w_gate, "dp", axis=0, tiled=True),
        lax.all_gather(w_up, "dp", axis=0, tiled=True),
        lax.all_gather(w_down, "dp", axis=0, tiled=True),
        lax.all_gather(mlp_gain, "dp", axis=0, tiled=True),
    )
    gain_two = gain_two.astype(jnp.float32)
    unit_two, scale_two = norm_parts(middle)
    normed_two = (unit_two * gain_two).astype(jnp.bfloat16)
    gate = jnp.dot(normed_two, gate_full, preferred_element_type=jnp.float32)
    upward = jnp.dot(normed_two, up_full, preferred_element_type=jnp.float32)
    sigma = jax.nn.sigmoid(gate)
    active = (gate * sigma * upward).astype(jnp.bfloat16)
    mlp_out = lax.psum(dot_last(active, down_full).astype(jnp.bfloat16), "tensor").astype(
        jnp.float32
    )
    output = (middle + mlp_out).astype(jnp.bfloat16)
    gate_back, up_back, down_back, gain_back = (
        lax.all_gather(w_gate, "dp", axis=0, tiled=True),
        lax.all_gather(w_up, "dp", axis=0, tiled=True),
        lax.all_gather(w_down, "dp", axis=0, tiled=True),
        lax.all_gather(mlp_gain, "dp", axis=0, tiled=True),
    )
    gain_back = gain_back.astype(jnp.float32)
    down_grad = dot_first(out_grad, active)
    active_grad = jnp.dot(out_grad, down_back, preferred_element_type=jnp.float32)
    gate_delta = (active_grad * upward * sigma * (1.0 + gate * (1.0 - sigma))).astype(jnp.bfloat16)
    up_delta = (active_grad * gate * sigma).astype(jnp.bfloat16)
    gate_grad = dot_first(normed_two, gate_delta)
    up_grad = dot_first(normed_two, up_delta)
    normed_two_grad = lax.psum(
        dot_last(gate_delta, gate_back) + dot_last(up_delta, up_back), "tensor"
    )
    middle_part, mlp_gain_grad = norm_back(normed_two_grad, unit_two, scale_two, gain_back)
    middle_grad = out_grad.astype(jnp.float32) + middle_part
    query_back, key_back, value_back, out_back, gain_first = (
        lax.all_gather(w_query, "dp", axis=0, tiled=True),
        lax.all_gather(w_key, "dp", axis=0, tiled=True),
        lax.all_gather(w_value, "dp", axis=0, tiled=True),
        lax.all_gather(w_out, "dp", axis=0, tiled=True),
        lax.all_gather(attn_gain, "dp", axis=0, tiled=True),
    )
    gain_first = gain_first.astype(jnp.float32)
    attn_delta = middle_grad.astype(jnp.bfloat16)
    out_proj_grad = dot_first(attn_delta, attended)
    head_delta = (
        jnp.dot(attn_delta, out_back, preferred_element_type=jnp.float32)
        .astype(jnp.bfloat16)
        .reshape(length, kv_local, group, HEAD_DIM)
    )
    rescored = jnp.where(
        allowed,
        jnp.einsum("qhgd,khd->hgqk", query_group, key_rot, preferred_element_type=jnp.float32)
        * factor,
        masked_score,
    )
    probs = jnp.exp(rescored - log_total)
    prob_grad = jnp.einsum(
        "qhgd,khd->hgqk", head_delta, value_heads, preferred_element_type=jnp.float32
    )
    row_total = jnp.sum(probs * prob_grad, axis=-1, keepdims=True)
    score_delta = (probs * (prob_grad - row_total)).astype(jnp.bfloat16)
    query_rot_grad = (
        jnp.einsum("hgqk,khd->qhgd", score_delta, key_rot, preferred_element_type=jnp.float32)
        * factor
    )
    key_rot_grad = (
        jnp.einsum("hgqk,qhgd->khd", score_delta, query_group, preferred_element_type=jnp.float32)
        * factor
    )
    value_delta = (
        jnp.einsum(
            "hgqk,qhgd->khd",
            probs.astype(jnp.bfloat16),
            head_delta,
            preferred_element_type=jnp.float32,
        )
        .astype(jnp.bfloat16)
        .reshape(length, -1)
    )
    query_delta = (
        rotate(query_rot_grad.reshape(length, -1, HEAD_DIM), cosine, -sine)
        .astype(jnp.bfloat16)
        .reshape(length, -1)
    )
    key_delta = rotate(key_rot_grad, cosine, -sine).astype(jnp.bfloat16).reshape(length, -1)
    query_grad = dot_first(normed_one, query_delta)
    key_grad = dot_first(normed_one, key_delta)
    value_grad = dot_first(normed_one, value_delta)
    local_first = (
        dot_last(query_delta, query_back)
        + dot_last(key_delta, key_back)
        + dot_last(value_delta, value_back)
    )
    normed_one_grad = lax.psum(local_first.astype(jnp.bfloat16), "tensor").astype(jnp.float32)
    input_part, attn_gain_grad = norm_back(normed_one_grad, unit_one, scale_one, gain_first)
    input_grad = middle_grad + input_part
    (
        query_grad,
        key_grad,
        value_grad,
        out_proj_grad,
        gate_grad,
        up_grad,
        down_grad,
        attn_gain_grad,
        mlp_gain_grad,
    ) = (
        lax.psum_scatter(query_grad, "dp", scatter_dimension=0, tiled=True),
        lax.psum_scatter(key_grad, "dp", scatter_dimension=0, tiled=True),
        lax.psum_scatter(value_grad, "dp", scatter_dimension=0, tiled=True),
        lax.psum_scatter(out_proj_grad, "dp", scatter_dimension=0, tiled=True),
        lax.psum_scatter(gate_grad, "dp", scatter_dimension=0, tiled=True),
        lax.psum_scatter(up_grad, "dp", scatter_dimension=0, tiled=True),
        lax.psum_scatter(down_grad, "dp", scatter_dimension=0, tiled=True),
        lax.psum_scatter(attn_gain_grad, "dp", scatter_dimension=0, tiled=True),
        lax.psum_scatter(mlp_gain_grad, "dp", scatter_dimension=0, tiled=True),
    )
    return (
        output,
        input_grad,
        query_grad,
        key_grad,
        value_grad,
        out_proj_grad,
        gate_grad,
        up_grad,
        down_grad,
        attn_gain_grad,
        mlp_gain_grad,
    )


def solution(mesh):
    in_specs = (
        P("dp", None),
        P("dp"),
        P("dp"),
        P("dp", "tensor"),
        P("dp", "tensor"),
        P("dp", "tensor"),
        P("dp", "tensor"),
        P("dp", "tensor"),
        P("dp", "tensor"),
        P("dp", "tensor"),
        P("dp"),
        P("dp"),
        P("dp", None),
    )
    out_specs = (
        P("dp", None),
        P("dp", None),
        P("dp", "tensor"),
        P("dp", "tensor"),
        P("dp", "tensor"),
        P("dp", "tensor"),
        P("dp", "tensor"),
        P("dp", "tensor"),
        P("dp", "tensor"),
        P("dp"),
        P("dp"),
    )
    return jax.shard_map(
        on_device, mesh=mesh, in_specs=in_specs, out_specs=out_specs, check_vma=False
    )
```

profile of v0, /device:TPU:0, one launch (start us, length us, event | category | flops | bytes accessed | tf_op | source)
XLA Modules:
  0.0 2104.6 jit_solution(7362402371754869214)
XLA Ops:
  10.7 23.3 %all-gather = bf16[16,1,128]{2,1,0:T(2,128)(2,1)S(1)} all-gather(bf16[1,1,128]{2,1,0:T(2,128)(2,1)} %bitcast.134), channel_id=1, replica_groups=mesh['dp'=16,'tensor'=2] {'dp'}, dimensions={0}, use_global_device_ids=true | all-gather | bytes 4352 | tf_op jit(solution)/shard_map/all_gather | solution.py:87
  36.2 14.6 all-gather.10.cloned.1.call-done
  52.6 37.1 %all-gather.12.cloned.1.call-done = bf16[2048,256]{1,0:T(8,128)(2,1)} async-done(((bf16[128,256]{1,0:T(8,128)(2,1)}), bf16[2048,256]{1,0:T(8,128)(2,1)}) %all-gather.12.cloned.1.call-update) | async-done | bytes 1048592 | tf_op jit(solution)/shard_map/all_gather | solution.py:84
  91.8 49.5 %all-gather.14.cloned.1.call-done = bf16[2048,1024]{1,0:T(8,128)(2,1)} async-done(((bf16[128,1024]{1,0:T(8,128)(2,1)}), bf16[2048,1024]{1,0:T(8,128)(2,1)}) %all-gather.14.cloned.1.call-update) | async-done | bytes 4194320 | tf_op jit(solution)/shard_map/all_gather | solution.py:83
  141.3 4.0 fusion.36
  147.0 45.3 %all-gather.16.cloned.1.call-done = bf16[2048,1024]{1,0:T(8,128)(2,1)} async-done(((bf16[128,1024]{1,0:T(8,128)(2,1)}), bf16[2048,1024]{1,0:T(8,128)(2,1)}) %all-gather.16.cloned.1.call-update) | async-done | bytes 4194320 | tf_op jit(solution)/shard_map/all_gather | solution.py:86
  192.3 4.7 fusion.42
  199.1 19.5 all-gather.1
  218.6 17.2 all-reduce.8.cloned.1.call-done
  237.4 126.8 %all-gather.20.cloned.1.call-done = bf16[2048,4096]{1,0:T(8,128)(2,1)} async-done(((bf16[128,4096]{1,0:T(8,128)(2,1)}), bf16[2048,4096]{1,0:T(8,128)(2,1)}) %all-gather.20.cloned.1.call-update) | async-done | bytes 16777232 | tf_op jit(solution)/shard_map/all_gather | solution.py:133
  364.3 9.4 fusion.44
  373.7 117.4 %all-gather.18.cloned.1.call-done = bf16[2048,4096]{1,0:T(8,128)(2,1)} async-done(((bf16[128,4096]{1,0:T(8,128)(2,1)}), bf16[2048,4096]{1,0:T(8,128)(2,1)}) %all-gather.18.cloned.1.call-update) | async-done | bytes 16777232 | tf_op jit(solution)/shard_map/all_gather | solution.py:132
  491.1 9.4 fusion.43
  500.5 117.4 %all-gather.22.cloned.1.call-done = bf16[2048,4096]{1,0:T(8,128)(2,1)} async-done(((bf16[128,4096]{1,0:T(8,128)(2,1)}), bf16[2048,4096]{1,0:T(8,128)(2,1)}) %all-gather.22.cloned.1.call-update) | async-done | bytes 16777232 | tf_op jit(solution)/shard_map/all_gather | solution.py:134
  617.9 11.9 multiply_convert_fusion
  629.8 13.2 fusion.45
  643.0 12.9 convolution_add_fusion.1
  656.0 12.5 convolution_convert_fusion
  668.6 25.8 %all-reduce.10.cloned.1.call-done = f32[128,2048]{1,0:T(8,128)} async-done(((f32[128,2048]{1,0:T(8,128)}), f32[128,2048]{1,0:T(8,128)}) %all-reduce.10.cloned.1.call-update) | async-done | bytes 1048592 | tf_op jit(solution)/shard_map/psum | solution.py:161
  709.1 17.1 convolution_bitcast_fusion
  731.4 5.5 fusion.22
  737.5 4.7 fusion.34
  742.3 14.3 fusion.49
  757.0 21.0 fusion.48
  781.5 63.1 %all-reduce.2 = (f32[2048]{0:T(1024)S(1)}, f32[2048]{0:T(1024)S(1)}) all-reduce(f32[2048]{0:T(1024)S(1)} %get-tuple-element.46, f32[2048]{0:T(1024)S(1)} %get-tuple-element.44), channel_id=9, replica_groups=mesh['dp'=16,'tensor'=2] {'dp'}, use_global_device_ids=true, to_apply=%region_19.20.clone | all-reduce | flops 4096 | bytes 32768
  848.6 235.4 %reduce-scatter.20.cloned.1.call-done = f32[128,4096]{0,1:T(8,128)} async-done(((f32[2048,4096]{0,1:T(8,128)}), f32[128,4096]{0,1:T(8,128)}) %reduce-scatter.20.cloned.1.call-update) | async-done | bytes 2097168 | tf_op jit(solution)/shard_map/reduce_scatter | solution.py:245
  1086.8 62.2 %reduce-scatter.10.cloned.1.call-done = f32[128,256]{1,0:T(8,128)} async-done(((f32[2048,256]{1,0:T(8,128)}), f32[128,256]{1,0:T(8,128)}) %reduce-scatter.10.cloned.1.call-update) | async-done | bytes 131088 | tf_op jit(solution)/shard_map/reduce_scatter | solution.py:240
  1149.0 65.0 %reduce-scatter.12.cloned.1.call-done = f32[128,256]{1,0:T(8,128)} async-done(((f32[2048,256]{1,0:T(8,128)}), f32[128,256]{1,0:T(8,128)}) %reduce-scatter.12.cloned.1.call-update) | async-done | bytes 131088 | tf_op jit(solution)/shard_map/reduce_scatter | solution.py:241
  1214.1 106.9 %reduce-scatter.14.cloned.1.call-done = f32[128,1024]{1,0:T(8,128)} async-done(((f32[2048,1024]{1,0:T(8,128)}), f32[128,1024]{1,0:T(8,128)}) %reduce-scatter.14.cloned.1.call-update) | async-done | bytes 524304 | tf_op jit(solution)/shard_map/reduce_scatter | solution.py:242
  1321.0 107.6 %reduce-scatter.8.cloned.1.call-done = f32[128,1024]{1,0:T(8,128)} async-done(((f32[2048,1024]{1,0:T(8,128)}), f32[128,1024]{1,0:T(8,128)}) %reduce-scatter.8.cloned.1.call-update) | async-done | bytes 524304 | tf_op jit(solution)/shard_map/reduce_scatter | solution.py:239
  1428.6 334.9 %reduce-scatter.18.cloned.1.call-done = f32[128,4096]{1,0:T(8,128)} async-done(((f32[2048,4096]{1,0:T(8,128)}), f32[128,4096]{1,0:T(8,128)}) %reduce-scatter.18.cloned.1.call-update) | async-done | bytes 2097168 | tf_op jit(solution)/shard_map/reduce_scatter | solution.py:244
  1763.5 334.3 %reduce-scatter.16.cloned.1.call-done = f32[128,4096]{1,0:T(8,128)} async-done(((f32[2048,4096]{1,0:T(8,128)}), f32[128,4096]{1,0:T(8,128)}) %reduce-scatter.16.cloned.1.call-update) | async-done | bytes 2097168 | tf_op jit(solution)/shard_map/reduce_scatter | solution.py:243
  (125 shorter events, 45.3 us)
Async XLA Ops:
  7.2 134.1 %copy-start = (bf16[128,2048]{1,0:T(8,128)(2,1)S(1)}, bf16[128,2048]{1,0:T(8,128)(2,1)}, u32[]{:S(2)}) copy-start(bf16[128,2048]{1,0:T(8,128)(2,1)} %param.13) | copy-start | bytes 1572868
  7.2 43.6 %all-gather.10.cloned.1.call-start = ((), (), s32[]{:S(2)}) async-start(), calls=%async_computation.7 | async-start | bytes 1114112 | tf_op jit(solution)/shard_map/all_gather | solution.py:85
  7.9 81.8 %all-gather.12.cloned.1.call-start = ((), (), s32[]{:S(2)}) async-start(), calls=%async_computation.8 | async-start | bytes 1114112 | tf_op jit(solution)/shard_map/all_gather | solution.py:84
  8.7 132.6 %all-gather.14.cloned.1.call-start = ((), (), s32[]{:S(2)}) async-start(), calls=%async_computation.9 | async-start | bytes 4456448 | tf_op jit(solution)/shard_map/all_gather | solution.py:83
  9.4 182.9 %all-gather.16.cloned.1.call-start = ((), (), s32[]{:S(2)}) async-start(), calls=%async_computation.10 | async-start | bytes 4456448 | tf_op jit(solution)/shard_map/all_gather | solution.py:86
  10.0 225.8 %all-reduce.8.cloned.1.call-start = ((), (), s32[]{:S(2)}) async-start(), calls=%async_computation.11 | async-start | bytes 2097152 | tf_op jit(solution)/shard_map/psum | solution.py:129
  35.2 110.1 %copy-start.18 = (f32[128]{0:T(128)}, f32[128]{0:T(128)S(1)}, u32[]{:S(2)}) copy-start(f32[128]{0:T(128)S(1)} %add_rsqrt_fusion.1) | copy-start | bytes 1540
  52.6 94.0 %copy-start.13 = (bf16[128,256]{0,1:T(8,128)(2,1)}, bf16[128,256]{0,1:T(8,128)(2,1)S(1)}, u32[]{:S(2)}) copy-start(bf16[128,256]{0,1:T(8,128)(2,1)S(1)} %copy.51) | copy-start | bytes 196612
  91.8 54.9 %copy-start.14 = (bf16[128,4,32]{0,2,1:T(8,128)(2,1)}, bf16[128,4,32]{0,2,1:T(8,128)(2,1)S(1)}, u32[]{:S(2)}) copy-start(bf16[128,4,32]{0,2,1:T(8,128)(2,1)S(1)} %get-tuple-element.63) | copy-start | bytes 98308
  91.8 54.8 %copy-start.16 = (bf16[128,4,32]{0,2,1:T(8,128)(2,1)}, bf16[128,4,32]{0,2,1:T(8,128)(2,1)S(1)}, u32[]{:S(2)}) copy-start(bf16[128,4,32]{0,2,1:T(8,128)(2,1)S(1)} %get-tuple-element.64) | copy-start | bytes 98308
  146.4 50.6 %copy-start.2 = (f32[4,4,128,128]{2,3,1,0:T(8,128)}, f32[4,4,128,128]{2,3,1,0:T(8,128)S(1)}, u32[]{:S(2)}) copy-start(f32[4,4,128,128]{2,3,1,0:T(8,128)S(1)} %get-tuple-element.69) | copy-start | bytes 3145732
  147.0 51.4 %copy-start.6 = (bf16[4,64,4,128]{3,1,2,0:T(8,128)(2,1)}, bf16[4,64,4,128]{3,1,2,0:T(8,128)(2,1)S(1)}, u32[]{:S(2)}) copy-start(bf16[4,64,4,128]{3,1,2,0:T(8,128)(2,1)S(1)} %convolution_convert_fusion.1) | copy-start | bytes 786436
  192.3 6.9 copy-start.20
  197.0 167.3 %all-gather.20.cloned.1.call-start = ((), (), s32[]{:S(2)}) async-start(), calls=%async_computation.13 | async-start | bytes 17825792 | tf_op jit(solution)/shard_map/all_gather | solution.py:133
  197.6 293.5 %all-gather.18.cloned.1.call-start = ((), (), s32[]{:S(2)}) async-start(), calls=%async_computation.12 | async-start | bytes 17825792 | tf_op jit(solution)/shard_map/all_gather | solution.py:132
  198.3 419.5 %all-gather.22.cloned.1.call-start = ((), (), s32[]{:S(2)}) async-start(), calls=%async_computation.14 | async-start | bytes 17825792 | tf_op jit(solution)/shard_map/all_gather | solution.py:134
  199.1 495.3 %all-reduce.10.cloned.1.call-start = ((), (), s32[]{:S(2)}) async-start(), calls=%async_computation.15 | async-start | bytes 2097152 | tf_op jit(solution)/shard_map/psum | solution.py:161
  629.8 26.3 %copy-start.5 = (bf16[128,4096]{1,0:T(8,128)(2,1)}, bf16[128,4096]{1,0:T(8,128)(2,1)S(1)}, u32[]{:S(2)}) copy-start(bf16[128,4096]{1,0:T(8,128)(2,1)S(1)} %get-tuple-element.56) | copy-start | bytes 3145732
  655.9 123.9 %all-reduce.12.cloned.1.call-start = ((), (), s32[]{:S(2)}) async-start(), calls=%async_computation.23 | async-start | bytes 2097152 | tf_op jit(solution)/shard_map/psum | solution.py:144
  694.4 3.4 copy-start.4
  700.4 3.4 copy-start.3
  700.4 3.7 copy-start.10
  700.4 3.7 copy-start.12
  700.5 4.0 copy-start.15
  700.5 4.0 copy-start.17
  708.8 375.1 %reduce-scatter.20.cloned.1.call-start = ((), (), s32[]{:S(2)}) async-start(), calls=%async_computation.22 | async-start | bytes 35651584 | tf_op jit(solution)/shard_map/reduce_scatter | solution.py:245
  726.2 422.8 %reduce-scatter.10.cloned.1.call-start = ((), (), s32[]{:S(2)}) async-start(), calls=%async_computation.17 | async-start | bytes 2228224 | tf_op jit(solution)/shard_map/reduce_scatter | solution.py:240
  728.8 485.3 %reduce-scatter.12.cloned.1.call-start = ((), (), s32[]{:S(2)}) async-start(), calls=%async_computation.18 | async-start | bytes 2228224 | tf_op jit(solution)/shard_map/reduce_scatter | solution.py:241
  731.4 589.6 %reduce-scatter.14.cloned.1.call-start = ((), (), s32[]{:S(2)}) async-start(), calls=%async_computation.19 | async-start | bytes 8912896 | tf_op jit(solution)/shard_map/reduce_scatter | solution.py:242
  736.9 691.7 %reduce-scatter.8.cloned.1.call-start = ((), (), s32[]{:S(2)}) async-start(), calls=%async_computation.16 | async-start | bytes 8912896 | tf_op jit(solution)/shard_map/reduce_scatter | solution.py:239
  742.2 1021.3 %reduce-scatter.18.cloned.1.call-start = ((), (), s32[]{:S(2)}) async-start(), calls=%async_computation.21 | async-start | bytes 35651584 | tf_op jit(solution)/shard_map/reduce_scatter | solution.py:244
  756.7 1341.2 %reduce-scatter.16.cloned.1.call-start = ((), (), s32[]{:S(2)}) async-start(), calls=%async_computation.20 | async-start | bytes 35651584 | tf_op jit(solution)/shard_map/reduce_scatter | solution.py:243
  (7 other events, 9.5 us)
Sparse Core Ops, SparseCore 0:
  10.2 40.5 all-gather.9
  52.9 36.7 all-gather.11
  91.9 49.3 all-gather.13
  143.3 48.8 all-gather.15
  197.1 38.6 all-reduce.7
  237.8 126.4 all-gather.19
  366.4 124.5 all-gather.17
  493.2 124.5 all-gather.21
  656.1 38.2 all-reduce.9
  708.9 40.0 all-reduce.11
  753.3 330.5 reduce-scatter.19
  1088.1 60.8 reduce-scatter.9
  1153.3 60.6 reduce-scatter.11
  1218.6 102.3 reduce-scatter.13
  1325.5 103.0 reduce-scatter.7
  1433.3 330.1 reduce-scatter.17
  1768.2 329.6 reduce-scatter.15
where the time goes:
time: 2110 us; the launch traced here: 2100 us
  waiting for transfers between devices  1800 us (85%)
  matrix products  159 us (8%)
  blocking collectives  106 us (5%)
    reduce_scatter x1, waiting for transfers between devices, on_device(): lax.psum_scatter(up_grad, 'dp', scatter_dimension=0, tiled=True)  335 us
    reduce_scatter x1, waiting for transfers between devices, on_device(): lax.psum_scatter(gate_grad, 'dp', scatter_dimension=0, tiled=True)  334 us
    reduce_scatter x1, waiting for transfers between devices, on_device(): lax.psum_scatter(down_grad, 'dp', scatter_dimension=0, tiled=True)  235 us
    all_gather x1, waiting for transfers between devices, on_device(): lax.all_gather(w_up, 'dp', axis=0, tiled=True)  127 us
    all_gather x1, waiting for transfers between devices, on_device(): lax.all_gather(w_down, 'dp', axis=0, tiled=True)  117 us
    all_gather x1, waiting for transfers between devices, on_device(): lax.all_gather(w_gate, 'dp', axis=0, tiled=True)  117 us
    reduce_scatter x1, waiting for transfers between devices, on_device(): lax.psum_scatter(query_grad, 'dp', scatter_dimension=0, tiled=True)  108 us
    reduce_scatter x1, waiting for transfers between devices, on_device(): lax.psum_scatter(out_proj_grad, 'dp', scatter_dimension=0, tiled=True)  107 us
  transfers between devices with their start and end apart: 17, of which 16 were waited for; matrix products, arithmetic and copies ran while one was open for 6% of the time, Pallas kernels for 0%

commit v1 on v0

--- a/solution.py
+++ b/solution.py
@@ -10,6 +10,19 @@
 norm_eps = 1e-05
 rope_base = 500000.0
 masked_score = -1e30
+
+
+def wait_rings(obj):
+    mid_arr, n_now, last = (lax.axis_size("dp"), lax.axis_index("dp"), obj.shape[0])
+    xs_all = [(to_i, (to_i + 1) % mid_arr) for to_i in range(mid_arr)]
+    newest = jnp.zeros((*obj.shape[:0], mid_arr * last, *obj.shape[1:]), obj.dtype)
+    parts_out = obj
+    for i in range(mid_arr):
+        arr_out = (n_now - i) % mid_arr
+        newest = lax.dynamic_update_slice_in_dim(newest, parts_out, arr_out * last, axis=0)
+        if i < mid_arr - 1:
+            parts_out = lax.ppermute(parts_out, "dp", xs_all)
+    return newest
 
 
 def rope_freqs(head_dim):
@@ -83,7 +96,7 @@
         lax.all_gather(w_query, "dp", axis=0, tiled=True),
         lax.all_gather(w_key, "dp", axis=0, tiled=True),
         lax.all_gather(w_value, "dp", axis=0, tiled=True),
-        lax.all_gather(w_out, "dp", axis=0, tiled=True),
+        wait_rings(w_out),
         lax.all_gather(attn_gain, "dp", axis=0, tiled=True),
     )
     gain_one = gain_one.astype(jnp.float32)

time: 2110 us -> 2140 us (1.014)
  waiting for transfers between devices: 1800 us -> 1830 us
    ppermute x0 -> x15, waiting for transfers between devices: none -> 119 us  [wait_rings(): parts_out = lax.ppermute(parts_out, 'dp', xs_all)]
    all_gather x1, waiting for transfers between devices: 49.5 us -> 0.01 us  [on_device(): lax.all_gather(w_query, 'dp', axis=0, tiled=True)]
    all_gather x1, waiting for transfers between devices: 37.1 us -> 0.01 us  [on_device(): lax.all_gather(w_key, 'dp', axis=0, tiled=True)]
  transfers between devices with their start and end apart: 17 -> 32, of which waited for: 16 -> 27; matrix products, arithmetic and copies ran while one was open for 6% -> 6% of each run, Pallas kernels for 0% -> 0%
where the time goes in v1:
time: 2140 us
  waiting for transfers between devices  1830 us (86%)
  matrix products  157 us (7%)
  blocking collectives  96.4 us (5%)
  local copies, waits for them, and re-layouts  24.8 us (1%)
    reduce_scatter x1, waiting for transfers between devices, on_device(): lax.psum_scatter(up_grad, 'dp', scatter_dimension=0, tiled=True)  335 us
    reduce_scatter x1, waiting for transfers between devices, on_device(): lax.psum_scatter(gate_grad, 'dp', scatter_dimension=0, tiled=True)  334 us
    reduce_scatter x1, waiting for transfers between devices, on_device(): lax.psum_scatter(down_grad, 'dp', scatter_dimension=0, tiled=True)  238 us
    all_gather x1, waiting for transfers between devices, on_device(): lax.all_gather(w_gate, 'dp', axis=0, tiled=True)  127 us
    ppermute x15, waiting for transfers between devices, wait_rings(): parts_out = lax.ppermute(parts_out, 'dp', xs_all)  119 us
    all_gather x1, waiting for transfers between devices, on_device(): lax.all_gather(w_down, 'dp', axis=0, tiled=True)  117 us
    all_gather x1, waiting for transfers between devices, on_device(): lax.all_gather(w_up, 'dp', axis=0, tiled=True)  117 us
    reduce_scatter x1, waiting for transfers between devices, on_device(): lax.psum_scatter(out_proj_grad, 'dp', scatter_dimension=0, tiled=True)  108 us
  transfers between devices with their start and end apart: 32, of which 27 were waited for; matrix products, arithmetic and copies ran while one was open for 6% of the time, Pallas kernels for 0%

profile of v1, /device:TPU:0, one launch (start us, length us, event | category | flops | bytes accessed | tf_op | source)
XLA Modules:
  0.0 2136.8 jit_solution(2617676982825267050)
XLA Ops:
  10.0 9.2 collective-permute-done
  19.2 9.4 collective-permute-done.1
  28.6 8.5 collective-permute-done.2
  37.1 11.1 collective-permute-done.3
  74.5 17.9 all-gather
  107.1 11.4 collective-permute-done.9
  129.1 11.4 collective-permute-done.11
  141.3 9.7 collective-permute-done.12
  182.5 17.7 all-gather.1
  200.2 17.8 all-reduce.8.cloned.1.call-done
  219.7 126.8 %all-gather.16.cloned.1.call-done = bf16[2048,4096]{1,0:T(8,128)(2,1)} async-done(((bf16[128,4096]{1,0:T(8,128)(2,1)}), bf16[2048,4096]{1,0:T(8,128)(2,1)}) %all-gather.16.cloned.1.call-update) | async-done | bytes 16777232 | tf_op jit(solution)/shard_map/all_gather | solution.py:145
  346.5 9.4 fusion.43
  356.0 117.2 %all-gather.18.cloned.1.call-done = bf16[2048,4096]{1,0:T(8,128)(2,1)} async-done(((bf16[128,4096]{1,0:T(8,128)(2,1)}), bf16[2048,4096]{1,0:T(8,128)(2,1)}) %all-gather.18.cloned.1.call-update) | async-done | bytes 16777232 | tf_op jit(solution)/shard_map/all_gather | solution.py:146
  473.2 9.4 fusion.44
  482.6 117.4 %all-gather.20.cloned.1.call-done = bf16[2048,4096]{1,0:T(8,128)(2,1)} async-done(((bf16[128,4096]{1,0:T(8,128)(2,1)}), bf16[2048,4096]{1,0:T(8,128)(2,1)}) %all-gather.20.cloned.1.call-update) | async-done | bytes 16777232 | tf_op jit(solution)/shard_map/all_gather | solution.py:147
  600.0 11.9 multiply_convert_fusion
  611.9 13.2 fusion.45
  625.1 12.9 convolution_add_fusion.1
  638.9 12.5 convolution_convert_fusion
  651.4 25.1 %all-reduce.10.cloned.1.call-done = f32[128,2048]{1,0:T(8,128)} async-done(((f32[128,2048]{1,0:T(8,128)}), f32[128,2048]{1,0:T(8,128)}) %all-reduce.10.cloned.1.call-update) | async-done | bytes 1048592 | tf_op jit(solution)/shard_map/psum | solution.py:174
  680.4 48.7 %all-gather.22.cloned.1.call-done = bf16[2048,1024]{1,0:T(8,128)(2,1)} async-done(((bf16[128,1024]{1,0:T(8,128)(2,1)}), bf16[2048,1024]{1,0:T(8,128)(2,1)}) %all-gather.22.cloned.1.call-update) | async-done | bytes 4194320 | tf_op jit(solution)/shard_map/all_gather | solution.py:183
  742.4 17.1 convolution_bitcast_fusion
  774.3 14.4 fusion.49
  789.0 21.0 fusion.48
  813.4 60.9 %all-reduce.2 = (f32[2048]{0:T(1024)S(1)}, f32[2048]{0:T(1024)S(1)}) all-reduce(f32[2048]{0:T(1024)S(1)} %get-tuple-element.46, f32[2048]{0:T(1024)S(1)} %copy-done.20), channel_id=9, replica_groups=mesh['dp'=16,'tensor'=2] {'dp'}, use_global_device_ids=true, to_apply=%region_19.20.clone | all-reduce | flops 4096 | bytes 32768
  878.3 237.9 %reduce-scatter.20.cloned.1.call-done = f32[128,4096]{0,1:T(8,128)} async-done(((f32[2048,4096]{0,1:T(8,128)}), f32[128,4096]{0,1:T(8,128)}) %reduce-scatter.20.cloned.1.call-update) | async-done | bytes 2097168 | tf_op jit(solution)/shard_map/reduce_scatter | solution.py:258
  1119.0 62.2 %reduce-scatter.10.cloned.1.call-done = f32[128,256]{1,0:T(8,128)} async-done(((f32[2048,256]{1,0:T(8,128)}), f32[128,256]{1,0:T(8,128)}) %reduce-scatter.10.cloned.1.call-update) | async-done | bytes 131088 | tf_op jit(solution)/shard_map/reduce_scatter | solution.py:253
  1181.2 65.1 %reduce-scatter.12.cloned.1.call-done = f32[128,256]{1,0:T(8,128)} async-done(((f32[2048,256]{1,0:T(8,128)}), f32[128,256]{1,0:T(8,128)}) %reduce-scatter.12.cloned.1.call-update) | async-done | bytes 131088 | tf_op jit(solution)/shard_map/reduce_scatter | solution.py:254
  1246.3 106.9 %reduce-scatter.8.cloned.1.call-done = f32[128,1024]{1,0:T(8,128)} async-done(((f32[2048,1024]{1,0:T(8,128)}), f32[128,1024]{1,0:T(8,128)}) %reduce-scatter.8.cloned.1.call-update) | async-done | bytes 524304 | tf_op jit(solution)/shard_map/reduce_scatter | solution.py:252
  1353.2 107.6 %reduce-scatter.14.cloned.1.call-done = f32[128,1024]{1,0:T(8,128)} async-done(((f32[2048,1024]{1,0:T(8,128)}), f32[128,1024]{1,0:T(8,128)}) %reduce-scatter.14.cloned.1.call-update) | async-done | bytes 524304 | tf_op jit(solution)/shard_map/reduce_scatter | solution.py:255
  1460.8 334.9 %reduce-scatter.18.cloned.1.call-done = f32[128,4096]{1,0:T(8,128)} async-done(((f32[2048,4096]{1,0:T(8,128)}), f32[128,4096]{1,0:T(8,128)}) %reduce-scatter.18.cloned.1.call-update) | async-done | bytes 2097168 | tf_op jit(solution)/shard_map/reduce_scatter | solution.py:257
  1795.7 334.3 %reduce-scatter.16.cloned.1.call-done = f32[128,4096]{1,0:T(8,128)} async-done(((f32[2048,4096]{1,0:T(8,128)}), f32[128,4096]{1,0:T(8,128)}) %reduce-scatter.16.cloned.1.call-update) | async-done | bytes 2097168 | tf_op jit(solution)/shard_map/reduce_scatter | solution.py:256
  (178 shorter events, 129.9 us)
Async XLA Ops:
  7.2 111.4 %all-gather.10.cloned.1.call-start = ((), (), s32[]{:S(2)}) async-start(), calls=%async_computation.7 | async-start | bytes 1114112 | tf_op jit(solution)/shard_map/all_gather | solution.py:98
  7.9 119.3 %all-gather.12.cloned.1.call-start = ((), (), s32[]{:S(2)}) async-start(), calls=%async_computation.8 | async-start | bytes 1114112 | tf_op jit(solution)/shard_map/all_gather | solution.py:97
  8.7 160.1 %all-gather.14.cloned.1.call-start = ((), (), s32[]{:S(2)}) async-start(), calls=%async_computation.9 | async-start | bytes 4456448 | tf_op jit(solution)/shard_map/all_gather | solution.py:96
  9.4 208.7 %all-reduce.8.cloned.1.call-start = ((), (), s32[]{:S(2)}) async-start(), calls=%async_computation.10 | async-start | bytes 2097152 | tf_op jit(solution)/shard_map/psum | solution.py:142
  9.5 9.8 collective-permute-start
  19.2 9.4 collective-permute-start.1
  28.6 8.5 collective-permute-start.2
  37.1 11.1 collective-permute-start.3
  48.2 8.5 collective-permute-start.4
  56.7 8.6 collective-permute-start.5
  65.3 8.9 collective-permute-start.6
  74.2 22.3 %collective-permute-start.7 = (bf16[128,1024]{1,0:T(8,128)(2,1)S(1)}, bf16[128,1024]{1,0:T(8,128)(2,1)S(1)}, u32[]{:S(2)}, u32[]{:S(2)}) collective-permute-start(bf16[128,1024]{1,0:T(8,128)(2,1)S(1)} %collective-permute-done.6), channel_id=1, source_target_pairs={{0,2},{2,4},{4,6},{6,8},{8,10},{10,12},{12,14},{14,16},{16,18},{18... | collective-permute-start | bytes 786440 | tf_op jit(solution)/shard_map/ppermute | solution.py:24
  96.4 8.5 collective-permute-start.8
  105.0 13.6 collective-permute-start.9
  118.6 8.7 collective-permute-start.10
  127.3 13.2 collective-permute-start.11
  140.5 10.5 collective-permute-start.12
  151.0 8.5 collective-permute-start.13
  159.5 8.5 collective-permute-start.14
  180.6 166.0 %all-gather.16.cloned.1.call-start = ((), (), s32[]{:S(2)}) async-start(), calls=%async_computation.11 | async-start | bytes 17825792 | tf_op jit(solution)/shard_map/all_gather | solution.py:145
  181.2 292.0 %all-gather.18.cloned.1.call-start = ((), (), s32[]{:S(2)}) async-start(), calls=%async_computation.12 | async-start | bytes 17825792 | tf_op jit(solution)/shard_map/all_gather | solution.py:146
  181.7 418.2 %all-gather.20.cloned.1.call-start = ((), (), s32[]{:S(2)}) async-start(), calls=%async_computation.13 | async-start | bytes 17825792 | tf_op jit(solution)/shard_map/all_gather | solution.py:147
  182.5 494.0 %all-reduce.10.cloned.1.call-start = ((), (), s32[]{:S(2)}) async-start(), calls=%async_computation.14 | async-start | bytes 2097152 | tf_op jit(solution)/shard_map/psum | solution.py:174
  638.1 91.0 %all-gather.22.cloned.1.call-start = ((), (), s32[]{:S(2)}) async-start(), calls=%async_computation.15 | async-start | bytes 4456448 | tf_op jit(solution)/shard_map/all_gather | solution.py:183
  638.8 173.1 %all-reduce.12.cloned.1.call-start = ((), (), s32[]{:S(2)}) async-start(), calls=%async_computation.23 | async-start | bytes 2097152 | tf_op jit(solution)/shard_map/psum | solution.py:157
  742.1 374.0 %reduce-scatter.20.cloned.1.call-start = ((), (), s32[]{:S(2)}) async-start(), calls=%async_computation.22 | async-start | bytes 35651584 | tf_op jit(solution)/shard_map/reduce_scatter | solution.py:258
  759.5 421.7 %reduce-scatter.10.cloned.1.call-start = ((), (), s32[]{:S(2)}) async-start(), calls=%async_computation.17 | async-start | bytes 2228224 | tf_op jit(solution)/shard_map/reduce_scatter | solution.py:253
  762.1 484.2 %reduce-scatter.12.cloned.1.call-start = ((), (), s32[]{:S(2)}) async-start(), calls=%async_computation.18 | async-start | bytes 2228224 | tf_op jit(solution)/shard_map/reduce_scatter | solution.py:254
  764.0 589.2 %reduce-scatter.8.cloned.1.call-start = ((), (), s32[]{:S(2)}) async-start(), calls=%async_computation.16 | async-start | bytes 8912896 | tf_op jit(solution)/shard_map/reduce_scatter | solution.py:252
  768.7 692.1 %reduce-scatter.14.cloned.1.call-start = ((), (), s32[]{:S(2)}) async-start(), calls=%async_computation.19 | async-start | bytes 8912896 | tf_op jit(solution)/shard_map/reduce_scatter | solution.py:255
  774.2 1021.5 %reduce-scatter.18.cloned.1.call-start = ((), (), s32[]{:S(2)}) async-start(), calls=%async_computation.21 | async-start | bytes 35651584 | tf_op jit(solution)/shard_map/reduce_scatter | solution.py:257
  788.7 1341.3 %reduce-scatter.16.cloned.1.call-start = ((), (), s32[]{:S(2)}) async-start(), calls=%async_computation.20 | async-start | bytes 35651584 | tf_op jit(solution)/shard_map/reduce_scatter | solution.py:256
  (25 other events, 503.7 us)
Sparse Core Ops, SparseCore 0:
  10.2 41.8 all-gather.9
  54.2 38.9 all-gather.11
  95.4 53.7 all-gather.13
  180.7 37.3 all-reduce.7
  220.1 126.4 all-gather.15
  348.5 124.5 all-gather.17
  475.3 124.5 all-gather.19
  638.2 38.2 all-reduce.9
  678.7 50.3 all-gather.21
  742.2 38.6 all-reduce.11
  785.2 330.9 reduce-scatter.19
  1120.3 60.8 reduce-scatter.9
  1185.5 60.7 reduce-scatter.11
  1250.8 102.3 reduce-scatter.7
  1357.7 103.0 reduce-scatter.13
  1465.5 330.1 reduce-scatter.17
  1800.3 329.5 reduce-scatter.15
